TPU v7x, 32 devices: a whole 2x2x4 slice. The times are simulated.
32 devices in a mesh: cuts: 4 (over y, x), det: 2 (over core), bank: 4 (over z).
Axes of the slice: x: 2, y: 2, z: 4, core: 2. Of those that a mesh axis runs over, the one named last changes fastest.
Arguments:
- strain: bfloat16 [4, 2, 6144], P('cuts', 'det'), may hold values from -6 to 6
- filters: bfloat16 [16, 256, 2048], P(('bank', 'cuts')), parts along dimension 0, may hold values from -0.125 to 0.125
- recon_weights: bfloat16 [16, 128, 256], P(('bank', 'cuts')), parts along dimension 0, may hold values from -0.1875 to 0.1875
- row_spans: int32 [512], P('bank'), parts along dimension 0, may hold values from 1 to 4
- slice_rates: int32 [4], replicated, may hold values from 1 to 8, as said below
- delays: int32 [64, 2], replicated, may hold values from 0 to 47
- antenna: float32 [64, 2], replicated, may hold values from 0.2 to 1
Outputs:
- peak_amplitude: float32 [512, 4096], P(('bank', 'cuts', 'det')), parts along dimension 0
There are 4 independent parts, one for each index of `bank`. A program takes and returns all parts, laid end to end along the dimension named above; an argument that names none is the same for every part. Nothing has to cross between parts.
Inputs may be any that keep to these rules, and one draw needn't show every extreme that they name: `slice_rates`: every entry is a power of two; entries never fall along the slices; the first is 1 and the last is 8.
All inputs are finite; a program needn't handle non-finite values.
Results may differ from a plain program's by a relative error of at most 0.0014.
Values sent between devices are 32-bit elements; how exact they have to be, the bound alone decides.
A program may use at most 64 MiB of HBM per device.

v0:
```python
import functools

import jax
import jax.numpy as jnp
from jax import lax
from jax.experimental import pallas as pl
from jax.experimental.pallas import tpu as pltpu
from jax.sharding import PartitionSpec as P

MESH = pl.DeviceIdType.MESH
LANES = 128
WIDE = 256
BATCH = 2
COARSEST = 8
CHUNK = 64
EARLY = 2
GRANT = 16 * 2**20


def partner(me, step):
    bit, other = 1, me
    while bit <= step:
        if step & bit:
            other = other + bit * (1 - 2 * lax.rem(lax.div(me, bit), 2))
        bit *= 2
    return other


def stack(bank, pieces):
    taps = bank.astype(jnp.bfloat16)
    return jnp.concatenate([taps[:, piece * WIDE : (piece + 1) * WIDE] for piece in range(pieces)], axis=0)


def convolve(stacked, fetch, dets, pieces, chunks, batches, even, odd, last, total):
    rows = stacked.shape[0] // pieces
    ahead = lax.broadcasted_iota(jnp.int32, (LANES, LANES), 1) >= lax.broadcasted_iota(
        jnp.int32, (LANES, LANES), 0
    )

    def build(keep, first, previous=None):
        for det in range(dets):
            if previous is not None:
                keep[det, 0] = previous[det, 2 * BATCH]
                before = last[det].astype(jnp.float32)
            for near in range(1, 2 * BATCH + 1):
                at = pl.multiple_of(jnp.minimum(first + near + 1, chunks - 1) * LANES, LANES)
                piece = fetch(det, at)
                now = pltpu.roll(jnp.broadcast_to(piece, (LANES, LANES)), 0, 1, stride=1, stride_axis=0)
                if previous is not None or near > 1:
                    keep[det, near] = jnp.where(ahead, now, before).astype(jnp.bfloat16)
                before = now
            last[det] = before.astype(jnp.bfloat16)

    def multiply(keep, det, sums, start):
        for near in range(BATCH):
            low, middle, high = keep[det, 2 * near], keep[det, 2 * near + 1], keep[det, 2 * near + 2]
            square = jnp.concatenate(
                [jnp.concatenate([middle, high], axis=1), jnp.concatenate([low, middle], axis=1)], axis=0
            )
            result = jnp.dot(stacked, square, preferred_element_type=jnp.float32)
            for piece in range(pieces):
                term = result[piece * rows : (piece + 1) * rows]
                old = sums[start + near + piece]
                sums[start + near + piece] = term if old is None else old + term

    for det in range(dets):
        for near in range(2):
            even[det, near] = jnp.zeros((LANES, LANES), jnp.bfloat16)
        for at in range(2 * pieces - 2):
            total[det, at] = jnp.zeros((rows, LANES), jnp.float32)
    build(even, -2)

    def one_batch(batch, carry):
        base = 2 * BATCH * batch
        sums = [[None] * (2 * BATCH + pieces - 1) for det in range(dets)]
        build(odd, 2 * base + 2 * BATCH - 2, even)
        for det in range(dets):
            multiply(even, det, sums[det], 0)
        build(even, 2 * base + 4 * BATCH - 2, odd)
        for det in range(dets):
            multiply(odd, det, sums[det], BATCH)
            for far, value in enumerate(sums[det]):
                for half in range(2):
                    at = 2 * (base + far) + half
                    part = value[:, half * LANES : (half + 1) * LANES]
                    total[det, at] = part if far >= pieces - 1 else total[det, at] + part
        return carry

    lax.fori_loop(0, batches, one_batch, 0)


def batches_of(blocks, pieces):
    return (blocks + pieces + 2 * BATCH - 1) // (2 * BATCH)


def exchange_kernel(
    cuts, dets, early,
    spans_hbm, strain_hbm, weights_hbm, filters_hbm, rates_hbm, delays_hbm, antenna_hbm,
    bank_ref, series_ref, partial_ref, rates_ref, delays_ref, antenna_ref,
    spans_ref, strain_ref, weights_ref, filters, bank_stage, bank_early, series, even, odd, last,
    bank_send, bank_recv, cross_send, cross_recv, side_send, side_recv,
    local_sem,
):
    me = lax.axis_index("cuts")
    core = lax.axis_index("det")
    barrier = pltpu.get_barrier_semaphore()
    for step in range(1, cuts):
        pl.semaphore_signal(
            barrier, inc=1, device_id={"cuts": partner(me, step)}, device_id_type=MESH
        )
    for turn in range(1, dets):
        pl.semaphore_signal(
            barrier, inc=1, device_id={"det": lax.rem(core + turn, dets)}, device_id_type=MESH
        )

    fetches = [
        pltpu.make_async_copy(strain_hbm, strain_ref, local_sem.at[0]),
        pltpu.make_async_copy(spans_hbm, spans_ref, local_sem.at[1]),
        pltpu.make_async_copy(weights_hbm, weights_ref, local_sem.at[2]),
        pltpu.make_async_copy(filters_hbm, filters, local_sem.at[3]),
        pltpu.make_async_copy(rates_hbm, rates_ref, local_sem.at[4]),
        pltpu.make_async_copy(delays_hbm, delays_ref, local_sem.at[5]),
        pltpu.make_async_copy(antenna_hbm, antenna_ref, local_sem.at[6]),
    ]
    for copy in fetches:
        copy.start()

    def series_at(step, det):
        if step <= early:
            return series.at[step * dets + det]
        return series_ref.at[(step - early - 1) * dets + det]

    def bank_at(step):
        return bank_early.at[step - 1] if step <= early else bank_ref.at[step - early - 1]

    fetches[0].wait()
    series[core] = strain_ref[...].astype(jnp.float32)
    pl.semaphore_wait(barrier, cuts - 1 + dets - 1)
    cross = []
    for step in range(1, cuts):
        cross.append(pltpu.make_async_remote_copy(
            src_ref=series_at(0, core), dst_ref=series_at(step, core),
            send_sem=cross_send.at[step - 1], recv_sem=cross_recv.at[step - 1],
            device_id={"cuts": partner(me, step)}, device_id_type=MESH,
        ))
    side = []
    for step in range(cuts):
        for turn in range(1, dets):
            number = step * (dets - 1) + turn - 1
            side.append(pltpu.make_async_remote_copy(
                src_ref=series_at(step, core), dst_ref=series_at(step, core),
                send_sem=side_send.at[number], recv_sem=side_recv.at[number],
                device_id={"det": lax.rem(core + turn, dets)}, device_id_type=MESH,
            ))
    for copy in cross:
        copy.start()
    for copy in side[: dets - 1]:
        copy.start()

    fetches[1].wait()
    fetches[2].wait()
    rows = weights_ref.shape[0]
    share = rows // cuts // dets
    live = (me < spans_ref[...]).astype(jnp.float32)
    across = lax.broadcasted_iota(jnp.int32, (rows, rows), 1)
    down = lax.broadcasted_iota(jnp.int32, (rows, rows), 0)
    keep = jnp.sum(jnp.where(across == down, live, 0.0), axis=1, keepdims=True)
    kept = (weights_ref[...].astype(jnp.float32) * keep).astype(jnp.bfloat16)
    parts = []
    for cut in range(cuts):
        low = kept[(cut * dets) * share : (cut * dets + 1) * share]
        for det in range(1, dets):
            other = kept[(cut * dets + det) * share : (cut * dets + det + 1) * share]
            low = jnp.where(core == det, other, low)
        parts.append(low)
    stacked = jnp.concatenate(parts, axis=0)
    fetches[3].wait()
    taps = filters.shape[1]
    for first in range(0, taps, WIDE):
        block = jnp.dot(stacked, filters[:, first : first + WIDE], preferred_element_type=jnp.float32)
        for cut in range(cuts):
            bank_stage[cut, :, first : first + WIDE] = block[cut * share : (cut + 1) * share]
    banks = []
    for step in range(1, cuts):
        target = partner(me, step)
        banks.append(pltpu.make_async_remote_copy(
            src_ref=bank_stage.at[target], dst_ref=bank_at(step),
            send_sem=bank_send.at[step - 1], recv_sem=bank_recv.at[step - 1],
            device_id={"cuts": target}, device_id_type=MESH,
        ))
    for copy in banks:
        copy.start()

    pieces = taps // WIDE
    length = series.shape[2]
    window = length - taps

    def filtered(step, bank):
        blocks = jnp.where(partner(me, step) == cuts - 1, window // COARSEST // WIDE, window // WIDE)
        convolve(
            stack(bank, pieces), lambda det, at: series[step * dets + det, :, pl.ds(at, LANES)],
            dets, pieces, length // LANES, lax.div(blocks + pieces + 2 * BATCH - 1, 2 * BATCH),
            even, odd, last, partial_ref.at[step],
        )

    for copy in side[: dets - 1]:
        copy.wait_recv()
    filtered(0, bank_stage[me])
    for step in range(1, cuts):
        cross[step - 1].wait_recv()
        for copy in side[step * (dets - 1) : (step + 1) * (dets - 1)]:
            copy.start()
    for step in range(1, early + 1):
        for copy in side[step * (dets - 1) : (step + 1) * (dets - 1)]:
            copy.wait_recv()
        banks[step - 1].wait_recv()
        filtered(step, bank_early[step - 1])
    for copy in fetches[4:]:
        copy.wait()
    for copy in side[(early + 1) * (dets - 1) :]:
        copy.wait_recv()
    for copy in banks[early:]:
        copy.wait_recv()
    for copy in cross + side + banks:
        copy.wait_send()


def total_tiles(length, taps):
    return length // LANES + 4 * BATCH + 2 * (taps // WIDE)


def exchange(spans, strain, filters, weights, rates, delays, antenna, cuts, dets, early):
    rows = weights.shape[0] // cuts // dets
    taps = filters.shape[1]
    length = strain.shape[-1]
    late = cuts - 1 - early
    hbm = pl.BlockSpec(memory_space=pltpu.HBM)
    free = pl.BlockSpec(memory_space=pl.ANY)
    vmem = pl.BlockSpec(memory_space=pltpu.VMEM)
    dma = pltpu.SemaphoreType.DMA
    square = (dets, 2 * BATCH + 1, LANES, LANES)
    return pl.pallas_call(
        functools.partial(exchange_kernel, cuts, dets, early),
        out_shape=(
            jax.ShapeDtypeStruct((late, rows, taps), jnp.float32),
            jax.ShapeDtypeStruct((late * dets, 1, length), jnp.float32),
            jax.ShapeDtypeStruct((1 + early, dets, total_tiles(length, taps), rows, LANES), jnp.float32),
            jax.ShapeDtypeStruct(rates.shape, rates.dtype),
            jax.ShapeDtypeStruct(delays.shape, delays.dtype),
            jax.ShapeDtypeStruct(antenna.shape, antenna.dtype),
        ),
        in_specs=[hbm] * 7,
        out_specs=(free, free, vmem, free, free, free),
        scratch_shapes=[
            pltpu.VMEM(spans.shape, spans.dtype),
            pltpu.VMEM(strain.shape, strain.dtype),
            pltpu.VMEM(weights.shape, weights.dtype),
            pltpu.VMEM(filters.shape, filters.dtype),
            pltpu.VMEM((cuts, rows, taps), jnp.float32),
            pltpu.VMEM((early, rows, taps), jnp.float32),
            pltpu.VMEM(((1 + early) * dets, 1, length), jnp.float32),
            pltpu.VMEM(square, jnp.bfloat16),
            pltpu.VMEM(square, jnp.bfloat16),
            pltpu.VMEM((dets, LANES, LANES), jnp.bfloat16),
            dma((cuts - 1,)),
            dma((cuts - 1,)),
            dma((cuts - 1,)),
            dma((cuts - 1,)),
            dma((cuts * (dets - 1),)),
            dma((cuts * (dets - 1),)),
            dma((7,)),
        ],
        compiler_params=pltpu.CompilerParams(collective_id=0, has_side_effects=True, vmem_limit_bytes=GRANT),
    )(*[pltpu.with_memory_space_constraint(x, pltpu.HBM)
        for x in (spans, strain, weights, filters, rates, delays, antenna)])


def search_kernel(
    early, rates_ref, delays_ref, antenna_ref, bank_ref, series_ref, partial_ref, peak_ref,
    even, odd, last, total, combined, turned, best,
):
    late, rows, taps = bank_ref.shape
    dets = series_ref.shape[0] // late
    window = peak_ref.shape[1]
    tiles = window // LANES
    pieces = taps // WIDE
    chunks = series_ref.shape[2] // LANES
    skip = 2 * pieces
    me = lax.axis_index("cuts")
    lane = lax.broadcasted_iota(jnp.int32, (rows, LANES), 1)

    def level_of(step):
        rate = rates_ref[me ^ step]
        return sum((rate >= 2**known).astype(jnp.int32) for known in range(1, COARSEST.bit_length()))

    def filtered(index):
        level = level_of(index + early + 1)
        blocks = lax.shift_right_logical(jnp.int32(window // WIDE), level)
        convolve(
            stack(bank_ref[index], pieces), lambda det, at: series_ref[index * dets + det, :, pl.ds(at, LANES)],
            dets, pieces, chunks, batches_of(blocks, pieces), even, odd, last, total,
        )
        return level

    def widen(level):
        narrow = lax.shift_right_logical(lane, level)
        width = lax.shift_right_logical(jnp.int32(LANES), level)
        rate = lax.shift_left(jnp.int32(1), level)

        def at(values, det, tile):
            index = narrow + (tile & (rate - 1)) * width
            source = values[det, skip + lax.shift_right_logical(jnp.int32(tile), level)]
            return jnp.take_along_axis(source, index, axis=1)

        return at

    if late > 1:
        for det in range(dets):
            for tile in range(tiles):
                combined[det, tile] = jnp.zeros((rows, LANES), jnp.float32)

        def one_slice(index, carry):
            at = widen(filtered(index))
            for tile in range(tiles):
                for det in range(dets):
                    combined[det, tile] += at(total, det, tile)
            return carry

        lax.fori_loop(0, late - 1, one_slice, 0)

    final = widen(filtered(late - 1))
    firsts = [widen(level_of(step)) for step in range(early + 1)]
    for tile in range(tiles):
        for det in range(dets):
            values = final(total, det, tile)
            for step, at in enumerate(firsts):
                values += at(partial_ref.at[step], det, tile)
            if late > 1:
                values += combined[det, tile]
            combined[det, tile] = values
    for det in range(dets):
        combined[det, tiles] = jnp.zeros((rows, LANES), jnp.float32)

    groups = LANES // rows
    apart = tiles // groups
    for det in range(dets):
        for offset in range(apart + 1):
            block = jnp.concatenate(
                [combined[det, group * apart + offset] for group in range(groups)], axis=0
            )
            turned[det, offset * LANES : (offset + 1) * LANES] = block.T

    for first in range(0, apart * LANES, CHUNK):
        def direction(number, highest):
            summed = None
            for det in range(dets):
                start = delays_ref[det, number] + first
                term = antenna_ref[det, number] * turned[det, pl.ds(start, CHUNK), :]
                summed = term if summed is None else summed + term
            return jnp.maximum(highest, jnp.abs(summed))

        best[first : first + CHUNK] = lax.fori_loop(
            0, delays_ref.shape[1], direction, jnp.zeros((CHUNK, LANES), jnp.float32), unroll=16
        )
    for offset in range(apart):
        back = best[offset * LANES : (offset + 1) * LANES].T
        for group in range(groups):
            at = (group * apart + offset) * LANES
            peak_ref[:, at : at + LANES] = back[group * rows : (group + 1) * rows]


def search(rates, delays, antenna, bank, series, partial, window, early):
    late, rows, taps = bank.shape
    dets = series.shape[0] // late
    tiles = window // LANES
    groups = LANES // rows
    apart = tiles // groups
    smem = pl.BlockSpec(memory_space=pltpu.SMEM)
    vmem = pl.BlockSpec(memory_space=pltpu.VMEM)
    square = (dets, 2 * BATCH + 1, LANES, LANES)
    return pl.pallas_call(
        functools.partial(search_kernel, early),
        out_shape=jax.ShapeDtypeStruct((rows, window), jnp.float32),
        in_specs=[smem, smem, smem, vmem, vmem, vmem],
        out_specs=vmem,
        scratch_shapes=[
            pltpu.VMEM(square, jnp.bfloat16),
            pltpu.VMEM(square, jnp.bfloat16),
            pltpu.VMEM((dets, LANES, LANES), jnp.bfloat16),
            pltpu.VMEM((dets, total_tiles(window + taps, taps), rows, LANES), jnp.float32),
            pltpu.VMEM((dets, tiles + 1, rows, LANES), jnp.float32),
            pltpu.VMEM((dets, (apart + 1) * LANES, LANES), jnp.float32),
            pltpu.VMEM((apart * LANES, LANES), jnp.float32),
        ],
        compiler_params=pltpu.CompilerParams(vmem_limit_bytes=GRANT),
    )(rates, delays, antenna, bank, series, partial)


def shards(strain, filters, recon_weights, row_spans, slice_rates, delays, antenna):
    cuts = lax.axis_size("cuts")
    dets = lax.axis_size("det")
    early = min(EARLY, cuts - 2)
    bank, series, partial, rates, delays, antenna = exchange(
        row_spans.reshape(1, -1), strain.reshape(1, -1), filters[0], recon_weights[0],
        slice_rates, delays.T, antenna.T, cuts, dets, early,
    )
    window = strain.shape[-1] - filters.shape[-1]
    return search(rates, delays, antenna, bank, series, partial, window, early)


def solution(mesh):
    placed = (
        P("cuts", "det", None),
        P(("bank", "cuts"), None, None),
        P(("bank", "cuts"), None, None),
        P("bank"),
        P(),
        P(),
        P(),
    )
    return jax.shard_map(
        shards,
        mesh=mesh,
        in_specs=placed,
        out_specs=P(("bank", "cuts", "det"), None),
        check_vma=False,
    )
```

profile of v0, /device:TPU:0, one launch (start us, length us, event | category | flops | bytes accessed | tf_op | source)
XLA Modules:
  0.0 22.4 jit_solution(6262768218015207541)
XLA Ops:
  0.0 15.0 %shard_map.73 = (f32[1,16,2048]{2,1,0:T(8,128)S(1)}, f32[2,1,6144]{2,1,0:T(1,128)S(1)}, f32[3,2,72,16,128]{4,3,2,1,0:T(8,128)S(1)}, s32[4]{0:T(128)S(1)}, s32[2,64]{1,0:T(2,128)S(1)}, /*index=5*/f32[2,64]{1,0:T(2,128)S(1)}) custom-call(s32[1,128]{1,0:T(1,128)} %bitcast.11, bf16[1,6144]{1,0:T(2,128)(2,1)} %bitcast.8, bf16[128,256]{1,0:T(8,128)(2,1)} %bitcast.7, ...), custom_call_target="tpu_custom_call" | custom-call | tf_op jit(solution)/shard_map/pallas_call | solution.py:242
  15.0 7.4 %shard_map.74 = f32[16,4096]{1,0:T(8,128)} custom-call(s32[4]{0:T(128)S(1)} %get-tuple-element.11.rates_ref, s32[2,64]{1,0:T(2,128)S(1)} %get-tuple-element.12.delays_ref, f32[2,64]{1,0:T(2,128)S(1)} %get-tuple-element.13.antenna_ref, f32[1,16,2048]{2,1,0:T(8,128)S(1)} %get-tuple-element.14.bank_ref, f32[2,1,6144]{2,1,0:T(1,128)S(1)} %get-tuple-element.15.series_ref, ...), custom_call_target="tpu_custom_call" | custom-call | tf_op jit(solution)/shard_map/pallas_call | solution.py:381
where the time goes:
time: 22.5 us; the launch traced here: 22.4 us
  Pallas kernels  22.4 us (100%)
    pallas_call x1, Pallas kernels, exchange(): pl.pallas_call(functools.partial(exchange_kernel, cuts, dets, early), out...  15 us
    pallas_call x1, Pallas kernels, search(): pl.pallas_call(functools.partial(search_kernel, early), out_shape=jax.Sha...  7.43 us

commit v1 on v0

v1 whole, which is shorter than its diff:
```python
import functools

import jax
import jax.numpy as jnp
from jax import lax
from jax.experimental import pallas as pl
from jax.experimental.pallas import tpu as pltpu
from jax.sharding import PartitionSpec as P

MESH = pl.DeviceIdType.MESH
LANES = 128
WIDE = 256
BATCH = 4
DEEP = 16
COARSEST = 8
HALO = 48
CHUNK = 64
EARLY = 1
READY = 2
GRANT = 24 * 2**20


def partner(me, step):
    bit, other = 1, me
    while bit <= step:
        if step & bit:
            other = other + bit * (1 - 2 * lax.rem(lax.div(me, bit), 2))
        bit *= 2
    return other


def batches_of(blocks, pieces):
    return (blocks + pieces - 1 + BATCH - 1) // BATCH


def total_tiles(length, taps):
    pieces = taps // WIDE
    return 2 * (BATCH * batches_of((length - taps) // WIDE, pieces) + pieces - 1)


def tile_count(length, taps):
    return 2 * BATCH * batches_of((length - taps) // WIDE, taps // WIDE) + 2


def fill(fetch, tiles, dets, chunks):
    deep = next(deep for deep in range(DEEP, 0, -1) if chunks % deep == 0)
    ahead = lax.broadcasted_iota(jnp.int32, (LANES, LANES), 1) >= lax.broadcasted_iota(
        jnp.int32, (LANES, LANES), 0
    )

    def some(number, carry):
        left = []
        for det, before in zip(dets, carry):
            for near in range(deep):
                chunk = number * deep + near
                piece = fetch(det, pl.multiple_of(chunk * LANES, LANES))
                now = pltpu.roll(jnp.broadcast_to(piece, (LANES, LANES)), 0, 1, stride=1, stride_axis=0)
                tiles[det, chunk] = jnp.where(ahead, now, before).astype(jnp.bfloat16)
                before = now
            left.append(before)
        return tuple(left)

    lax.fori_loop(0, chunks // deep, some, tuple(jnp.zeros((LANES, LANES), jnp.float32) for det in dets))


def stack(bank, pieces):
    taps = bank.astype(jnp.bfloat16)
    return jnp.concatenate([taps[:, piece * WIDE : (piece + 1) * WIDE] for piece in range(pieces)], axis=0)


def convolve(stacked, tiles, dets, pieces, batches, total):
    rows = stacked.shape[0] // pieces

    def one_batch(batch, carry):
        base = BATCH * batch
        for det in dets:
            sums = [None] * (BATCH + pieces - 1)
            for near in range(BATCH):
                first = 2 * (base + near) + 1
                low, middle, high = tiles[det, first], tiles[det, first + 1], tiles[det, first + 2]
                square = jnp.concatenate(
                    [jnp.concatenate([middle, high], axis=1), jnp.concatenate([low, middle], axis=1)], axis=0
                )
                result = jnp.dot(stacked, square, preferred_element_type=jnp.float32)
                for piece in range(pieces):
                    term = result[piece * rows : (piece + 1) * rows]
                    old = sums[near + piece]
                    sums[near + piece] = term if old is None else old + term
            for far, value in enumerate(sums):
                for half in range(2):
                    at = 2 * (base + far) + half
                    part = value[:, half * LANES : (half + 1) * LANES]
                    total[det, at] = part if far >= pieces - 1 else total[det, at] + part
        return carry

    lax.fori_loop(0, batches, one_batch, 0)


def exchange_kernel(
    cuts, dets, early, ready,
    spans_hbm, strain_hbm, weights_hbm, filters_hbm, rates_hbm, delays_hbm, antenna_hbm,
    bank_ref, series_ref, partial_ref, tiles_ref, rates_ref, delays_ref, antenna_ref,
    spans_ref, strain_ref, weights_ref, filters, bank_stage, bank_early, series, tiles,
    bank_send, bank_recv, cross_send, cross_recv, side_send, side_recv,
    local_sem,
):
    me = lax.axis_index("cuts")
    core = lax.axis_index("det")
    barrier = pltpu.get_barrier_semaphore()
    for step in range(1, cuts):
        pl.semaphore_signal(
            barrier, inc=1, device_id={"cuts": partner(me, step)}, device_id_type=MESH
        )
    for turn in range(1, dets):
        pl.semaphore_signal(
            barrier, inc=1, device_id={"det": lax.rem(core + turn, dets)}, device_id_type=MESH
        )

    fetches = [
        pltpu.make_async_copy(strain_hbm, strain_ref, local_sem.at[0]),
        pltpu.make_async_copy(spans_hbm, spans_ref, local_sem.at[1]),
        pltpu.make_async_copy(weights_hbm, weights_ref, local_sem.at[2]),
        pltpu.make_async_copy(filters_hbm, filters, local_sem.at[3]),
        pltpu.make_async_copy(rates_hbm, rates_ref, local_sem.at[4]),
        pltpu.make_async_copy(delays_hbm, delays_ref, local_sem.at[5]),
        pltpu.make_async_copy(antenna_hbm, antenna_ref, local_sem.at[6]),
    ]
    for copy in fetches:
        copy.start()
    held = early + ready

    def series_at(step, det):
        if step <= held:
            return series.at[step * dets + det]
        return series_ref.at[(step - held - 1) * dets + det]

    def bank_at(step):
        return bank_early.at[step - 1] if step <= early else bank_ref.at[step - early - 1]

    fetches[0].wait()
    series[core] = strain_ref[...].astype(jnp.float32)
    pl.semaphore_wait(barrier, cuts - 1 + dets - 1)
    cross = []
    for step in range(1, cuts):
        cross.append(pltpu.make_async_remote_copy(
            src_ref=series_at(0, core), dst_ref=series_at(step, core),
            send_sem=cross_send.at[step - 1], recv_sem=cross_recv.at[step - 1],
            device_id={"cuts": partner(me, step)}, device_id_type=MESH,
        ))
    side = []
    for step in range(cuts):
        for turn in range(1, dets):
            number = step * (dets - 1) + turn - 1
            side.append(pltpu.make_async_remote_copy(
                src_ref=series_at(step, core), dst_ref=series_at(step, core),
                send_sem=side_send.at[number], recv_sem=side_recv.at[number],
                device_id={"det": lax.rem(core + turn, dets)}, device_id_type=MESH,
            ))
    for copy in cross:
        copy.start()
    for copy in side[: dets - 1]:
        copy.start()

    fetches[1].wait()
    fetches[2].wait()
    rows = weights_ref.shape[0]
    share = rows // cuts // dets
    live = (me < spans_ref[...]).astype(jnp.float32)
    across = lax.broadcasted_iota(jnp.int32, (rows, rows), 1)
    down = lax.broadcasted_iota(jnp.int32, (rows, rows), 0)
    keep = jnp.sum(jnp.where(across == down, live, 0.0), axis=1, keepdims=True)
    kept = (weights_ref[...].astype(jnp.float32) * keep).astype(jnp.bfloat16)
    parts = []
    for cut in range(cuts):
        low = kept[(cut * dets) * share : (cut * dets + 1) * share]
        for det in range(1, dets):
            other = kept[(cut * dets + det) * share : (cut * dets + det + 1) * share]
            low = jnp.where(core == det, other, low)
        parts.append(low)
    stacked = jnp.concatenate(parts, axis=0)
    fetches[3].wait()
    taps = filters.shape[1]
    for first in range(0, taps, WIDE):
        block = jnp.dot(stacked, filters[:, first : first + WIDE], preferred_element_type=jnp.float32)
        for cut in range(cuts):
            bank_stage[cut, :, first : first + WIDE] = block[cut * share : (cut + 1) * share]
    banks = []
    for step in range(1, cuts):
        target = partner(me, step)
        banks.append(pltpu.make_async_remote_copy(
            src_ref=bank_stage.at[target], dst_ref=bank_at(step),
            send_sem=bank_send.at[step - 1], recv_sem=bank_recv.at[step - 1],
            device_id={"cuts": target}, device_id_type=MESH,
        ))
    for copy in banks:
        copy.start()

    pieces = taps // WIDE
    length = series.shape[2]
    window = length - taps
    chunks = length // LANES

    def prepare(step, which, out):
        fill(lambda det, at: series[step * dets + det, :, pl.ds(at, LANES)], out, which, chunks)

    def filtered(step, which, bank):
        full = batches_of(window // WIDE, pieces)
        short = batches_of(window // COARSEST // WIDE, pieces)
        batches = jnp.where(partner(me, step) == cuts - 1, short, full)
        convolve(stack(bank, pieces), tiles.at[step], which, pieces, batches, partial_ref.at[step])

    everyone = list(range(dets))
    prepare(0, [core], tiles.at[0])
    filtered(0, [core], bank_stage[me])
    for copy in side[: dets - 1]:
        copy.wait_recv()
    for turn in range(1, dets):
        other = lax.rem(core + turn, dets)
        prepare(0, [other], tiles.at[0])
        filtered(0, [other], bank_stage[me])
    for step in range(1, cuts):
        cross[step - 1].wait_recv()
        for copy in side[step * (dets - 1) : (step + 1) * (dets - 1)]:
            copy.start()
    for step in range(1, held + 1):
        for copy in side[step * (dets - 1) : (step + 1) * (dets - 1)]:
            copy.wait_recv()
        prepare(step, everyone, tiles.at[step] if step <= early else tiles_ref.at[step - early - 1])
    for step in range(1, early + 1):
        banks[step - 1].wait_recv()
        filtered(step, everyone, bank_early[step - 1])
    for copy in fetches[4:]:
        copy.wait()
    for copy in side[(held + 1) * (dets - 1) :]:
        copy.wait_recv()
    for copy in banks[early:]:
        copy.wait_recv()
    for copy in cross + side + banks:
        copy.wait_send()


def exchange(spans, strain, filters, weights, rates, delays, antenna, cuts, dets, early, ready):
    rows = weights.shape[0] // cuts // dets
    taps = filters.shape[1]
    length = strain.shape[-1]
    late = cuts - 1 - early
    rest = max(late - ready, 1)
    hbm = pl.BlockSpec(memory_space=pltpu.HBM)
    free = pl.BlockSpec(memory_space=pl.ANY)
    vmem = pl.BlockSpec(memory_space=pltpu.VMEM)
    dma = pltpu.SemaphoreType.DMA
    squares = (dets, tile_count(length, taps), LANES, LANES)
    return pl.pallas_call(
        functools.partial(exchange_kernel, cuts, dets, early, ready),
        out_shape=(
            jax.ShapeDtypeStruct((late, rows, taps), jnp.float32),
            jax.ShapeDtypeStruct((rest * dets, 1, length), jnp.float32),
            jax.ShapeDtypeStruct((1 + early, dets, total_tiles(length, taps), rows, LANES), jnp.float32),
            jax.ShapeDtypeStruct((ready, *squares), jnp.bfloat16),
            jax.ShapeDtypeStruct(rates.shape, rates.dtype),
            jax.ShapeDtypeStruct(delays.shape, delays.dtype),
            jax.ShapeDtypeStruct(antenna.shape, antenna.dtype),
        ),
        in_specs=[hbm] * 7,
        out_specs=(free, free, vmem, vmem, free, free, free),
        scratch_shapes=[
            pltpu.VMEM(spans.shape, spans.dtype),
            pltpu.VMEM(strain.shape, strain.dtype),
            pltpu.VMEM(weights.shape, weights.dtype),
            pltpu.VMEM(filters.shape, filters.dtype),
            pltpu.VMEM((cuts, rows, taps), jnp.float32),
            pltpu.VMEM((early, rows, taps), jnp.float32),
            pltpu.VMEM(((1 + early + ready) * dets, 1, length), jnp.float32),
            pltpu.VMEM((1 + early, *squares), jnp.bfloat16),
            dma((cuts - 1,)),
            dma((cuts - 1,)),
            dma((cuts - 1,)),
            dma((cuts - 1,)),
            dma((cuts * (dets - 1),)),
            dma((cuts * (dets - 1),)),
            dma((7,)),
        ],
        compiler_params=pltpu.CompilerParams(collective_id=0, has_side_effects=True, vmem_limit_bytes=GRANT),
    )(*[pltpu.with_memory_space_constraint(x, pltpu.HBM)
        for x in (spans, strain, weights, filters, rates, delays, antenna)])


def search_kernel(
    early, ready, rates_ref, delays_ref, antenna_ref, bank_ref, series_ref, partial_ref, tiles_ref, peak_ref,
    total, turned, best, *squares,
):
    late, rows, taps = bank_ref.shape
    dets = partial_ref.shape[1]
    window = peak_ref.shape[1]
    length = series_ref.shape[2]
    pieces = taps // WIDE
    skip = 2 * (pieces - 1)
    everyone = list(range(dets))
    me = lax.axis_index("cuts")

    groups = LANES // rows
    apart = window // LANES // groups
    span = apart * LANES
    split = max(1, COARSEST // apart)
    ways = groups // split
    group_at = [place % ways * split + place // ways for place in range(groups)]

    def level_of(step):
        rate = rates_ref[me ^ step]
        return sum((rate >= 2**known).astype(jnp.int32) for known in range(1, COARSEST.bit_length()))

    def filtered(index, tiles, level):
        blocks = lax.shift_right_logical(jnp.int32(window // WIDE), level)
        convolve(stack(bank_ref[index], pieces), tiles, everyone, pieces, batches_of(blocks, pieces), total)

    def widen(values, level):
        for known in range(COARSEST.bit_length()):
            @pl.when(level == known)
            def _(known=known):
                rate = 2**known
                per = apart // rate
                for det in range(dets):
                    blocks = []
                    for near in range(per):
                        block = jnp.concatenate(
                            [values[det, skip + group * per + near] for group in group_at], axis=0
                        )
                        blocks.append((near * LANES, block.T))
                    if not per:
                        block = jnp.concatenate([values[det, skip + way] for way in range(ways)], axis=0).T
                        part = LANES // split
                        blocks = [(0, jnp.concatenate(
                            [block[turn * part : (turn + 1) * part] for turn in range(split)], axis=1
                        ))]
                    for first, block in blocks:
                        size = block.shape[0]
                        for turn in range(rate):
                            if rate > 1:
                                place = pl.ds(first * rate + turn, size, stride=rate)
                            else:
                                place = pl.ds(first, size)
                            turned[det, place, :] += block

    for det in range(dets):
        turned[det] = jnp.zeros(turned.shape[1:], jnp.float32)
    for step in range(early + 1):
        widen(partial_ref.at[step], level_of(step))
    for index in range(ready):
        level = level_of(early + 1 + index)
        filtered(index, tiles_ref.at[index], level)
        widen(total, level)
    if late > ready:
        def one_slice(index, carry):
            level = level_of(early + 1 + index)
            fill(
                lambda det, at: series_ref[(index - ready) * dets + det, :, pl.ds(at, LANES)],
                squares[0], everyone, length // LANES,
            )
            filtered(index, squares[0], level)
            widen(total, level)
            return carry

        lax.fori_loop(ready, late, one_slice, 0)

    lane = lax.broadcasted_iota(jnp.int32, (HALO, LANES), 1)
    row, place = lane & (rows - 1), lane // rows
    group = (place & (ways - 1)) * split + place // ways
    later = jnp.minimum(group + 1, groups - 1)
    source = ((later & (split - 1)) * ways + later // split) * rows + row
    for det in range(dets):
        following = jnp.take_along_axis(turned[det, :HALO], source, axis=1)
        turned[det, span : span + HALO] = jnp.where(group == groups - 1, 0.0, following)

    for first in range(0, span, CHUNK):
        def direction(number, highest):
            summed = None
            for det in range(dets):
                start = delays_ref[det, number] + first
                term = antenna_ref[det, number] * turned[det, pl.ds(start, CHUNK), :]
                summed = term if summed is None else summed + term
            return jnp.maximum(highest, jnp.abs(summed))

        best[first : first + CHUNK] = lax.fori_loop(
            0, delays_ref.shape[1], direction, jnp.zeros((CHUNK, LANES), jnp.float32), unroll=16
        )
    for near in range(apart):
        back = best[near * LANES : (near + 1) * LANES].T
        for place, group in enumerate(group_at):
            at = (group * apart + near) * LANES
            peak_ref[:, at : at + LANES] = back[place * rows : (place + 1) * rows]


def search(rates, delays, antenna, bank, series, partial, tiles, window, early):
    late, rows, taps = bank.shape
    ready = tiles.shape[0]
    dets = partial.shape[1]
    span = window // (LANES // rows)
    smem = pl.BlockSpec(memory_space=pltpu.SMEM)
    vmem = pl.BlockSpec(memory_space=pltpu.VMEM)
    return pl.pallas_call(
        functools.partial(search_kernel, early, ready),
        out_shape=jax.ShapeDtypeStruct((rows, window), jnp.float32),
        in_specs=[smem, smem, smem, vmem, vmem, vmem, vmem],
        out_specs=vmem,
        scratch_shapes=[
            pltpu.VMEM(partial.shape[1:], jnp.float32),
            pltpu.VMEM((dets, span + HALO, LANES), jnp.float32),
            pltpu.VMEM((span, LANES), jnp.float32),
        ] + [pltpu.VMEM(tiles.shape[1:], tiles.dtype)] * (late > ready),
        compiler_params=pltpu.CompilerParams(vmem_limit_bytes=GRANT),
    )(rates, delays, antenna, bank, series, partial, tiles)


def shards(strain, filters, recon_weights, row_spans, slice_rates, delays, antenna):
    cuts = lax.axis_size("cuts")
    dets = lax.axis_size("det")
    early = min(EARLY, cuts - 2)
    ready = min(READY, cuts - 1 - early)
    bank, series, partial, tiles, rates, delays, antenna = exchange(
        row_spans.reshape(1, -1), strain.reshape(1, -1), filters[0], recon_weights[0],
        slice_rates, delays.T, antenna.T, cuts, dets, early, ready,
    )
    window = strain.shape[-1] - filters.shape[-1]
    return search(rates, delays, antenna, bank, series, partial, tiles, window, early)


def solution(mesh):
    placed = (
        P("cuts", "det", None),
        P(("bank", "cuts"), None, None),
        P(("bank", "cuts"), None, None),
        P("bank"),
        P(),
        P(),
        P(),
    )
    return jax.shard_map(
        shards,
        mesh=mesh,
        in_specs=placed,
        out_specs=P(("bank", "cuts", "det"), None),
        check_vma=False,
    )
```

time: 22.5 us -> 22.2 us (0.987)
  the two profiles are of different devices: /device:TPU:0 before, /device:TPU:1 now
where the time goes in v1:
time: 22.2 us; the launch traced here: 22.1 us
  Pallas kernels  22.1 us (100%)
    pallas_call x1, Pallas kernels, exchange(): pl.pallas_call(functools.partial(exchange_kernel, cuts, dets, early, read...  14.6 us
    pallas_call x1, Pallas kernels, search(): pl.pallas_call(functools.partial(search_kernel, early, ready), out_shape=...  7.47 us

profile of v1, /device:TPU:1, one launch (start us, length us, event | category | flops | bytes accessed | tf_op | source)
XLA Modules:
  0.0 22.1 jit_solution(5492522523216430858)
XLA Ops:
  0.0 14.6 %shard_map.73 = (f32[2,16,2048]{2,1,0:T(8,128)S(1)}, f32[2,1,6144]{2,1,0:T(1,128)S(1)}, f32[2,2,62,16,128]{4,3,2,1,0:T(8,128)S(1)}, bf16[2,2,50,128,128]{4,3,2,1...) custom-call(s32[1,128]{1,0:T(1,128)} %bitcast.11, bf16[1,6144]{1,0:T(2,128)(2,1)} %bitcast.8, ...), custom_call_target="tpu_custom_call" | custom-call | tf_op jit(solution)/shard_map/pallas_call | solution.py:253
  14.6 7.5 %shard_map.74 = f32[16,4096]{1,0:T(8,128)} custom-call(s32[4]{0:T(128)S(1)} %get-tuple-element.12.rates_ref, s32[2,64]{1,0:T(2,128)S(1)} %get-tuple-element.13.delays_ref, f32[2,64]{1,0:T(2,128)S(1)} %get-tuple-element.14.antenna_ref, f32[2,16,2048]{2,1,0:T(8,128)S(1)} %get-tuple-element.15.bank_ref, f32[2,1,6144]{2,1,0:T(1,128)S(1)} %get-tuple-element.16.series_ref, ...), custom_call_target="tpu_custom_call" | custom-call | tf_op jit(solution)/shard_map/pallas_call | solution.py:400

commit v2 on v1

--- a/solution.py
+++ b/solution.py
@@ -11,7 +11,7 @@
 LANES = 128
 WIDE = 256
 BATCH = 4
-DEEP = 16
+DEEP = 48
 COARSEST = 8
 HALO = 48
 CHUNK = 64
@@ -96,11 +96,77 @@
     lax.fori_loop(0, batches, one_batch, 0)
 
 
+def convolve_building(stacked, fetch, dets, pieces, chunks, batches, even, odd, last, total, between=None):
+    rows = stacked.shape[0] // pieces
+    half = BATCH // 2
+    ahead = lax.broadcasted_iota(jnp.int32, (LANES, LANES), 1) >= lax.broadcasted_iota(
+        jnp.int32, (LANES, LANES), 0
+    )
+
+    def shifted(det, chunk):
+        piece = fetch(det, pl.multiple_of(chunk * LANES, LANES))
+        return pltpu.roll(jnp.broadcast_to(piece, (LANES, LANES)), 0, 1, stride=1, stride_axis=0)
+
+    def build(keep, first, previous):
+        for det in dets:
+            keep[det, 0] = previous[det, 2 * half]
+            before = last[det].astype(jnp.float32)
+            for near in range(1, 2 * half + 1):
+                now = shifted(det, jnp.minimum(first + near, chunks - 1))
+                keep[det, near] = jnp.where(ahead, now, before).astype(jnp.bfloat16)
+                before = now
+            last[det] = before.astype(jnp.bfloat16)
+
+    def multiply(keep, det, sums, start):
+        for near in range(half):
+            low, middle, high = keep[det, 2 * near], keep[det, 2 * near + 1], keep[det, 2 * near + 2]
+            square = jnp.concatenate(
+                [jnp.concatenate([middle, high], axis=1), jnp.concatenate([low, middle], axis=1)], axis=0
+            )
+            result = jnp.dot(stacked, square, preferred_element_type=jnp.float32)
+            for piece in range(pieces):
+                term = result[piece * rows : (piece + 1) * rows]
+                old = sums[start + near + piece]
+                sums[start + near + piece] = term if old is None else old + term
+
+    for det in dets:
+        before = shifted(det, 0)
+        for near in range(2 * half + 1):
+            now = shifted(det, near + 1)
+            even[det, near] = jnp.where(ahead, now, before).astype(jnp.bfloat16)
+            before = now
+        last[det] = before.astype(jnp.bfloat16)
+
+    def one_batch(batch, carry):
+        base = BATCH * batch
+        sums = [[None] * (BATCH + pieces - 1) for det in dets]
+        build(odd, 2 * base + 2 * half + 1, even)
+        for det in dets:
+            multiply(even, det, sums[det], 0)
+        build(even, 2 * base + 4 * half + 1, odd)
+        for det in dets:
+            multiply(odd, det, sums[det], half)
+            for far, value in enumerate(sums[det]):
+                for side in range(2):
+                    at = 2 * (base + far) + side
+                    part = value[:, side * LANES : (side + 1) * LANES]
+                    total[det, at] = part if far >= pieces - 1 else total[det, at] + part
+        return carry
+
+    if between is None:
+        lax.fori_loop(0, batches, one_batch, 0)
+    else:
+        middle = lax.div(batches, 2)
+        lax.fori_loop(0, middle, one_batch, 0)
+        between()
+        lax.fori_loop(middle, batches, one_batch, 0)
+
+
 def exchange_kernel(
     cuts, dets, early, ready,
     spans_hbm, strain_hbm, weights_hbm, filters_hbm, rates_hbm, delays_hbm, antenna_hbm,
     bank_ref, series_ref, partial_ref, tiles_ref, rates_ref, delays_ref, antenna_ref,
-    spans_ref, strain_ref, weights_ref, filters, bank_stage, bank_early, series, tiles,
+    spans_ref, strain_ref, weights_ref, filters, bank_stage, bank_early, series, even, odd, last,
     bank_send, bank_recv, cross_send, cross_recv, side_send, side_recv,
     local_sem,
 ):
@@ -200,35 +266,51 @@
     window = length - taps
     chunks = length // LANES
 
-    def prepare(step, which, out):
-        fill(lambda det, at: series[step * dets + det, :, pl.ds(at, LANES)], out, which, chunks)
-
-    def filtered(step, which, bank):
-        full = batches_of(window // WIDE, pieces)
-        short = batches_of(window // COARSEST // WIDE, pieces)
-        batches = jnp.where(partner(me, step) == cuts - 1, short, full)
-        convolve(stack(bank, pieces), tiles.at[step], which, pieces, batches, partial_ref.at[step])
+    def fetch(step):
+        return lambda det, at: series[step * dets + det, :, pl.ds(at, LANES)]
+
+    full = batches_of(window // WIDE, pieces)
+    short = batches_of(window // COARSEST // WIDE, pieces)
+
+    def batches_at(step):
+        return jnp.where(partner(me, step) == cuts - 1, short, full)
+
+    def build(step, bank, between=None):
+        convolve_building(
+            stack(bank, pieces), fetch(step), everyone, pieces, chunks, batches_at(step),
+            even, odd, last, partial_ref.at[step], between,
+        )
+
+    def sides(step):
+        return side[step * (dets - 1) : (step + 1) * (dets - 1)]
+
+    def forward(step):
+        cross[step - 1].wait_recv()
+        for copy in sides(step):
+            copy.start()
+
+    def forward_first():
+        for step in range(1, early + 2):
+            forward(step)
 
     everyone = list(range(dets))
-    prepare(0, [core], tiles.at[0])
-    filtered(0, [core], bank_stage[me])
-    for copy in side[: dets - 1]:
+    for copy in sides(0):
         copy.wait_recv()
-    for turn in range(1, dets):
-        other = lax.rem(core + turn, dets)
-        prepare(0, [other], tiles.at[0])
-        filtered(0, [other], bank_stage[me])
-    for step in range(1, cuts):
-        cross[step - 1].wait_recv()
-        for copy in side[step * (dets - 1) : (step + 1) * (dets - 1)]:
-            copy.start()
-    for step in range(1, held + 1):
-        for copy in side[step * (dets - 1) : (step + 1) * (dets - 1)]:
+    build(0, bank_stage[me], forward_first)
+    for step in range(early + 2, cuts):
+        forward(step)
+    for step in range(early + 1, held + 1):
+        fill(fetch(step), tiles_ref.at[step - early - 1], [core], chunks)
+    for step in range(early + 1, held + 1):
+        for copy in sides(step):
             copy.wait_recv()
-        prepare(step, everyone, tiles.at[step] if step <= early else tiles_ref.at[step - early - 1])
+        for turn in range(1, dets):
+            fill(fetch(step), tiles_ref.at[step - early - 1], [lax.rem(core + turn, dets)], chunks)
     for step in range(1, early + 1):
+        for copy in sides(step):
+            copy.wait_recv()
         banks[step - 1].wait_recv()
-        filtered(step, everyone, bank_early[step - 1])
+        build(step, bank_early[step - 1])
     for copy in fetches[4:]:
         copy.wait()
     for copy in side[(held + 1) * (dets - 1) :]:
@@ -271,7 +353,9 @@
             pltpu.VMEM((cuts, rows, taps), jnp.float32),
             pltpu.VMEM((early, rows, taps), jnp.float32),
             pltpu.VMEM(((1 + early + ready) * dets, 1, length), jnp.float32),
-            pltpu.VMEM((1 + early, *squares), jnp.bfloat16),
+            pltpu.VMEM((dets, BATCH + 1, LANES, LANES), jnp.bfloat16),
+            pltpu.VMEM((dets, BATCH + 1, LANES, LANES), jnp.bfloat16),
+            pltpu.VMEM((dets, LANES, LANES), jnp.bfloat16),
             dma((cuts - 1,)),
             dma((cuts - 1,)),
             dma((cuts - 1,)),

time: 22.2 us -> 20.2 us (0.910)
  the two profiles are of different devices: /device:TPU:1 before, /device:TPU:0 now
where the time goes in v2:
time: 20.2 us; the launch traced here: 20 us
  Pallas kernels  20 us (99%)
    pallas_call x1, Pallas kernels, exchange(): pl.pallas_call(functools.partial(exchange_kernel, cuts, dets, early, read...  12.6 us
    pallas_call x1, Pallas kernels, search(): pl.pallas_call(functools.partial(search_kernel, early, ready), out_shape=...  7.4 us

profile of v2, /device:TPU:0, one launch (start us, length us, event | category | flops | bytes accessed | tf_op | source)
XLA Modules:
  0.0 20.0 jit_solution(11998407394852780327)
XLA Ops:
  0.0 12.6 %shard_map.73 = (f32[2,16,2048]{2,1,0:T(8,128)S(1)}, f32[2,1,6144]{2,1,0:T(1,128)S(1)}, f32[2,2,62,16,128]{4,3,2,1,0:T(8,128)S(1)}, bf16[2,2,50,128,128]{4,3,2,1...) custom-call(s32[1,128]{1,0:T(1,128)} %bitcast.11, bf16[1,6144]{1,0:T(2,128)(2,1)} %bitcast.8, ...), custom_call_target="tpu_custom_call" | custom-call | tf_op jit(solution)/shard_map/pallas_call | solution.py:335
  12.6 7.4 %shard_map.74 = f32[16,4096]{1,0:T(8,128)} custom-call(s32[4]{0:T(128)S(1)} %get-tuple-element.12.rates_ref, s32[2,64]{1,0:T(2,128)S(1)} %get-tuple-element.13.delays_ref, f32[2,64]{1,0:T(2,128)S(1)} %get-tuple-element.14.antenna_ref, f32[2,16,2048]{2,1,0:T(8,128)S(1)} %get-tuple-element.15.bank_ref, f32[2,1,6144]{2,1,0:T(1,128)S(1)} %get-tuple-element.16.series_ref, ...), custom_call_target="tpu_custom_call" | custom-call | tf_op jit(solution)/shard_map/pallas_call | solution.py:484

commit v3 on v1

--- a/solution.py
+++ b/solution.py
@@ -10,13 +10,13 @@
 MESH = pl.DeviceIdType.MESH
 LANES = 128
 WIDE = 256
-BATCH = 4
-DEEP = 16
+BATCH = 12
+DEEP = 48
 COARSEST = 8
 HALO = 48
 CHUNK = 64
-EARLY = 1
-READY = 2
+EARLY = 2
+READY = 1
 GRANT = 24 * 2**20
 
 
@@ -94,6 +94,28 @@
         return carry
 
     lax.fori_loop(0, batches, one_batch, 0)
+
+
+def convolve_flat(stacked, tiles, dets, pieces, blocks, total):
+    rows = stacked.shape[0] // pieces
+    for det in dets:
+        sums = [None] * blocks
+        for near in range(blocks + pieces - 1):
+            first = 2 * near + 1
+            low, middle, high = tiles[det, first], tiles[det, first + 1], tiles[det, first + 2]
+            square = jnp.concatenate(
+                [jnp.concatenate([middle, high], axis=1), jnp.concatenate([low, middle], axis=1)], axis=0
+            )
+            result = jnp.dot(stacked, square, preferred_element_type=jnp.float32)
+            for piece in range(pieces):
+                block = near + piece - (pieces - 1)
+                if 0 <= block < blocks:
+                    term = result[piece * rows : (piece + 1) * rows]
+                    sums[block] = term if sums[block] is None else sums[block] + term
+        for block, value in enumerate(sums):
+            for half in range(2):
+                at = 2 * (pieces - 1 + block) + half
+                total[det, at] = value[:, half * LANES : (half + 1) * LANES]
 
 
 def exchange_kernel(
@@ -200,35 +222,54 @@
     window = length - taps
     chunks = length // LANES
 
-    def prepare(step, which, out):
-        fill(lambda det, at: series[step * dets + det, :, pl.ds(at, LANES)], out, which, chunks)
-
-    def filtered(step, which, bank):
-        full = batches_of(window // WIDE, pieces)
-        short = batches_of(window // COARSEST // WIDE, pieces)
-        batches = jnp.where(partner(me, step) == cuts - 1, short, full)
-        convolve(stack(bank, pieces), tiles.at[step], which, pieces, batches, partial_ref.at[step])
+    def fetch(step):
+        return lambda det, at: series[step * dets + det, :, pl.ds(at, LANES)]
+
+    full = batches_of(window // WIDE, pieces)
+    short = batches_of(window // COARSEST // WIDE, pieces)
+
+    def batches_at(step):
+        return jnp.where(partner(me, step) == cuts - 1, short, full)
+
+    def filtered(step, bank):
+        out = tiles.at[step] if step <= early else tiles_ref.at[step - early - 1]
+        convolve(stack(bank, pieces), out, everyone, pieces, batches_at(step), partial_ref.at[step])
+
+    def prepare(step, det):
+        out = tiles.at[step] if step <= early else tiles_ref.at[step - early - 1]
+        fill(fetch(step), out, [det], chunks)
+
+    def sides(step):
+        return side[step * (dets - 1) : (step + 1) * (dets - 1)]
+
+    def forward(step):
+        cross[step - 1].wait_recv()
+        for copy in sides(step):
+            copy.start()
+
+    def prepare_others(step):
+        for copy in sides(step):
+            copy.wait_recv()
+        for turn in range(1, dets):
+            prepare(step, lax.rem(core + turn, dets))
 
     everyone = list(range(dets))
-    prepare(0, [core], tiles.at[0])
-    filtered(0, [core], bank_stage[me])
-    for copy in side[: dets - 1]:
-        copy.wait_recv()
-    for turn in range(1, dets):
-        other = lax.rem(core + turn, dets)
-        prepare(0, [other], tiles.at[0])
-        filtered(0, [other], bank_stage[me])
-    for step in range(1, cuts):
-        cross[step - 1].wait_recv()
-        for copy in side[step * (dets - 1) : (step + 1) * (dets - 1)]:
-            copy.start()
+    prepare(0, core)
+    prepare_others(0)
+    for step in range(1, early + 1):
+        forward(step)
+    filtered(0, bank_stage[me])
+    for step in range(1, early + 1):
+        prepare(step, core)
+    for step in range(early + 1, cuts):
+        forward(step)
+    for step in range(early + 1, held + 1):
+        prepare(step, core)
     for step in range(1, held + 1):
-        for copy in side[step * (dets - 1) : (step + 1) * (dets - 1)]:
-            copy.wait_recv()
-        prepare(step, everyone, tiles.at[step] if step <= early else tiles_ref.at[step - early - 1])
+        prepare_others(step)
     for step in range(1, early + 1):
         banks[step - 1].wait_recv()
-        filtered(step, everyone, bank_early[step - 1])
+        filtered(step, bank_early[step - 1])
     for copy in fetches[4:]:
         copy.wait()
     for copy in side[(held + 1) * (dets - 1) :]:
@@ -309,58 +350,60 @@
         rate = rates_ref[me ^ step]
         return sum((rate >= 2**known).astype(jnp.int32) for known in range(1, COARSEST.bit_length()))
 
-    def filtered(index, tiles, level):
-        blocks = lax.shift_right_logical(jnp.int32(window // WIDE), level)
-        convolve(stack(bank_ref[index], pieces), tiles, everyone, pieces, batches_of(blocks, pieces), total)
-
-    def widen(values, level):
+    def widen(values, known, fresh):
+        rate = 2**known
+        per = apart // rate
+        for det in range(dets):
+            blocks = []
+            for near in range(per):
+                block = jnp.concatenate(
+                    [values[det, skip + group * per + near] for group in group_at], axis=0
+                )
+                blocks.append((near * LANES, block.T))
+            if not per:
+                block = jnp.concatenate([values[det, skip + way] for way in range(ways)], axis=0).T
+                part = LANES // split
+                blocks = [(0, jnp.concatenate(
+                    [block[turn * part : (turn + 1) * part] for turn in range(split)], axis=1
+                ))]
+            for first, block in blocks:
+                size = block.shape[0]
+                for turn in range(rate):
+                    if rate > 1:
+                        place = pl.ds(first * rate + turn, size, stride=rate)
+                    else:
+                        place = pl.ds(first, size)
+                    if fresh:
+                        turned[det, place, :] = block
+                    else:
+                        turned[det, place, :] += block
+
+    def by_level(level, work):
         for known in range(COARSEST.bit_length()):
-            @pl.when(level == known)
-            def _(known=known):
-                rate = 2**known
-                per = apart // rate
-                for det in range(dets):
-                    blocks = []
-                    for near in range(per):
-                        block = jnp.concatenate(
-                            [values[det, skip + group * per + near] for group in group_at], axis=0
-                        )
-                        blocks.append((near * LANES, block.T))
-                    if not per:
-                        block = jnp.concatenate([values[det, skip + way] for way in range(ways)], axis=0).T
-                        part = LANES // split
-                        blocks = [(0, jnp.concatenate(
-                            [block[turn * part : (turn + 1) * part] for turn in range(split)], axis=1
-                        ))]
-                    for first, block in blocks:
-                        size = block.shape[0]
-                        for turn in range(rate):
-                            if rate > 1:
-                                place = pl.ds(first * rate + turn, size, stride=rate)
-                            else:
-                                place = pl.ds(first, size)
-                            turned[det, place, :] += block
-
-    for det in range(dets):
-        turned[det] = jnp.zeros(turned.shape[1:], jnp.float32)
+            pl.when(level == known)(functools.partial(work, known))
+
+    def one_slice(index, tiles):
+        def work(known):
+            blocks = window // WIDE // 2**known
+            convolve_flat(stack(bank_ref[index], pieces), tiles, everyone, pieces, blocks, total)
+            widen(total, known, False)
+
+        by_level(level_of(early + 1 + index), work)
+
     for step in range(early + 1):
-        widen(partial_ref.at[step], level_of(step))
+        by_level(level_of(step), functools.partial(widen, partial_ref.at[step], fresh=step == 0))
     for index in range(ready):
-        level = level_of(early + 1 + index)
-        filtered(index, tiles_ref.at[index], level)
-        widen(total, level)
+        one_slice(index, tiles_ref.at[index])
     if late > ready:
-        def one_slice(index, carry):
-            level = level_of(early + 1 + index)
+        def rest(index, carry):
             fill(
                 lambda det, at: series_ref[(index - ready) * dets + det, :, pl.ds(at, LANES)],
                 squares[0], everyone, length // LANES,
             )
-            filtered(index, squares[0], level)
-            widen(total, level)
+            one_slice(index, squares[0])
             return carry
 
-        lax.fori_loop(ready, late, one_slice, 0)
+        lax.fori_loop(ready, late, rest, 0)
 
     lane = lax.broadcasted_iota(jnp.int32, (HALO, LANES), 1)
     row, place = lane & (rows - 1), lane // rows

time: 22.2 us -> 19.3 us (0.87)
  the two profiles are of different devices: /device:TPU:1 before, /device:TPU:0 now
where the time goes in v3:
time: 19.3 us; the launch traced here: 19.2 us
  Pallas kernels  19.2 us (99%)
    pallas_call x1, Pallas kernels, exchange(): pl.pallas_call(functools.partial(exchange_kernel, cuts, dets, early, read...  13.1 us
    pallas_call x1, Pallas kernels, search(): pl.pallas_call(functools.partial(search_kernel, early, ready), out_shape=...  6.06 us

profile of v3, /device:TPU:0, one launch (start us, length us, event | category | flops | bytes accessed | tf_op | source)
XLA Modules:
  0.0 19.2 jit_solution(12193162348377933461)
XLA Ops:
  0.0 13.1 %shard_map.73 = (f32[1,16,2048]{2,1,0:T(8,128)S(1)}, f32[2,1,6144]{2,1,0:T(1,128)S(1)}, f32[3,2,62,16,128]{4,3,2,1,0:T(8,128)S(1)}, bf16[1,2,50,128,128]{4,3,2,1...) custom-call(s32[1,128]{1,0:T(1,128)} %bitcast.11, bf16[1,6144]{1,0:T(2,128)(2,1)} %bitcast.8, ...), custom_call_target="tpu_custom_call" | custom-call | tf_op jit(solution)/shard_map/pallas_call | solution.py:294
  13.1 6.1 %shard_map.74 = f32[16,4096]{1,0:T(8,128)} custom-call(s32[4]{0:T(128)S(1)} %get-tuple-element.12.rates_ref, s32[2,64]{1,0:T(2,128)S(1)} %get-tuple-element.13.delays_ref, f32[2,64]{1,0:T(2,128)S(1)} %get-tuple-element.14.antenna_ref, f32[1,16,2048]{2,1,0:T(8,128)S(1)} %get-tuple-element.15.bank_ref, f32[2,1,6144]{2,1,0:T(1,128)S(1)} %get-tuple-element.16.series_ref, ...), custom_call_target="tpu_custom_call" | custom-call | tf_op jit(solution)/shard_map/pallas_call | solution.py:443

commit v4 on v3

--- a/solution.py
+++ b/solution.py
@@ -10,7 +10,6 @@
 MESH = pl.DeviceIdType.MESH
 LANES = 128
 WIDE = 256
-BATCH = 12
 DEEP = 48
 COARSEST = 8
 HALO = 48
@@ -29,17 +28,8 @@
     return other
 
 
-def batches_of(blocks, pieces):
-    return (blocks + pieces - 1 + BATCH - 1) // BATCH
-
-
-def total_tiles(length, taps):
-    pieces = taps // WIDE
-    return 2 * (BATCH * batches_of((length - taps) // WIDE, pieces) + pieces - 1)
-
-
-def tile_count(length, taps):
-    return 2 * BATCH * batches_of((length - taps) // WIDE, taps // WIDE) + 2
+def tile_count(length):
+    return length // LANES
 
 
 def fill(fetch, tiles, dets, chunks):
@@ -68,39 +58,11 @@
     return jnp.concatenate([taps[:, piece * WIDE : (piece + 1) * WIDE] for piece in range(pieces)], axis=0)
 
 
-def convolve(stacked, tiles, dets, pieces, batches, total):
-    rows = stacked.shape[0] // pieces
-
-    def one_batch(batch, carry):
-        base = BATCH * batch
-        for det in dets:
-            sums = [None] * (BATCH + pieces - 1)
-            for near in range(BATCH):
-                first = 2 * (base + near) + 1
-                low, middle, high = tiles[det, first], tiles[det, first + 1], tiles[det, first + 2]
-                square = jnp.concatenate(
-                    [jnp.concatenate([middle, high], axis=1), jnp.concatenate([low, middle], axis=1)], axis=0
-                )
-                result = jnp.dot(stacked, square, preferred_element_type=jnp.float32)
-                for piece in range(pieces):
-                    term = result[piece * rows : (piece + 1) * rows]
-                    old = sums[near + piece]
-                    sums[near + piece] = term if old is None else old + term
-            for far, value in enumerate(sums):
-                for half in range(2):
-                    at = 2 * (base + far) + half
-                    part = value[:, half * LANES : (half + 1) * LANES]
-                    total[det, at] = part if far >= pieces - 1 else total[det, at] + part
-        return carry
-
-    lax.fori_loop(0, batches, one_batch, 0)
-
-
-def convolve_flat(stacked, tiles, dets, pieces, blocks, total):
+def convolve(stacked, tiles, dets, pieces, begin, end, blocks, total):
     rows = stacked.shape[0] // pieces
     for det in dets:
-        sums = [None] * blocks
-        for near in range(blocks + pieces - 1):
+        sums = {}
+        for near in range(begin, end):
             first = 2 * near + 1
             low, middle, high = tiles[det, first], tiles[det, first + 1], tiles[det, first + 2]
             square = jnp.concatenate(
@@ -111,11 +73,12 @@
                 block = near + piece - (pieces - 1)
                 if 0 <= block < blocks:
                     term = result[piece * rows : (piece + 1) * rows]
-                    sums[block] = term if sums[block] is None else sums[block] + term
-        for block, value in enumerate(sums):
+                    sums[block] = sums[block] + term if block in sums else term
+        for block, value in sums.items():
             for half in range(2):
-                at = 2 * (pieces - 1 + block) + half
-                total[det, at] = value[:, half * LANES : (half + 1) * LANES]
+                at = 2 * block + half
+                part = value[:, half * LANES : (half + 1) * LANES]
+                total[det, at] = part if begin <= block or not begin else total[det, at] + part
 
 
 def exchange_kernel(
@@ -225,15 +188,16 @@
     def fetch(step):
         return lambda det, at: series[step * dets + det, :, pl.ds(at, LANES)]
 
-    full = batches_of(window // WIDE, pieces)
-    short = batches_of(window // COARSEST // WIDE, pieces)
-
-    def batches_at(step):
-        return jnp.where(partner(me, step) == cuts - 1, short, full)
-
     def filtered(step, bank):
         out = tiles.at[step] if step <= early else tiles_ref.at[step - early - 1]
-        convolve(stack(bank, pieces), out, everyone, pieces, batches_at(step), partial_ref.at[step])
+        coarse = partner(me, step) == cuts - 1
+
+        def work(samples):
+            convolve(stack(bank, pieces), out, everyone, pieces, 0, samples // WIDE + pieces - 1, samples // WIDE,
+                     partial_ref.at[step])
+
+        pl.when(coarse)(functools.partial(work, window // COARSEST))
+        pl.when(jnp.logical_not(coarse))(functools.partial(work, window))
 
     def prepare(step, det):
         out = tiles.at[step] if step <= early else tiles_ref.at[step - early - 1]
@@ -290,13 +254,13 @@
     free = pl.BlockSpec(memory_space=pl.ANY)
     vmem = pl.BlockSpec(memory_space=pltpu.VMEM)
     dma = pltpu.SemaphoreType.DMA
-    squares = (dets, tile_count(length, taps), LANES, LANES)
+    squares = (dets, tile_count(length), LANES, LANES)
     return pl.pallas_call(
         functools.partial(exchange_kernel, cuts, dets, early, ready),
         out_shape=(
             jax.ShapeDtypeStruct((late, rows, taps), jnp.float32),
             jax.ShapeDtypeStruct((rest * dets, 1, length), jnp.float32),
-            jax.ShapeDtypeStruct((1 + early, dets, total_tiles(length, taps), rows, LANES), jnp.float32),
+            jax.ShapeDtypeStruct((1 + early, dets, (length - taps) // LANES, rows, LANES), jnp.float32),
             jax.ShapeDtypeStruct((ready, *squares), jnp.bfloat16),
             jax.ShapeDtypeStruct(rates.shape, rates.dtype),
             jax.ShapeDtypeStruct(delays.shape, delays.dtype),
@@ -327,15 +291,21 @@
 
 
 def search_kernel(
-    early, ready, rates_ref, delays_ref, antenna_ref, bank_ref, series_ref, partial_ref, tiles_ref, peak_ref,
-    total, turned, best, *squares,
+    early, ready, rates_any, delays_any, antenna_any, bank_ref, series_ref, partial_ref, tiles_ref, peak_ref,
+    rates_ref, delays_ref, antenna_ref, total, turned, best, table_sem, *squares,
 ):
+    tables = [
+        pltpu.make_async_copy(rates_any, rates_ref, table_sem.at[0]),
+        pltpu.make_async_copy(delays_any, delays_ref, table_sem.at[1]),
+        pltpu.make_async_copy(antenna_any, antenna_ref, table_sem.at[2]),
+    ]
+    for copy in tables:
+        copy.start()
     late, rows, taps = bank_ref.shape
     dets = partial_ref.shape[1]
     window = peak_ref.shape[1]
     length = series_ref.shape[2]
     pieces = taps // WIDE
-    skip = 2 * (pieces - 1)
     everyone = list(range(dets))
     me = lax.axis_index("cuts")
 
@@ -357,11 +327,11 @@
             blocks = []
             for near in range(per):
                 block = jnp.concatenate(
-                    [values[det, skip + group * per + near] for group in group_at], axis=0
+                    [values[det, group * per + near] for group in group_at], axis=0
                 )
                 blocks.append((near * LANES, block.T))
             if not per:
-                block = jnp.concatenate([values[det, skip + way] for way in range(ways)], axis=0).T
+                block = jnp.concatenate([values[det, way] for way in range(ways)], axis=0).T
                 part = LANES // split
                 blocks = [(0, jnp.concatenate(
                     [block[turn * part : (turn + 1) * part] for turn in range(split)], axis=1
@@ -382,25 +352,38 @@
         for known in range(COARSEST.bit_length()):
             pl.when(level == known)(functools.partial(work, known))
 
-    def one_slice(index, tiles):
+    fewest = window // WIDE // COARSEST + pieces - 1
+
+    def begin_slice(index, tiles):
+        convolve(stack(bank_ref[index], pieces), tiles, everyone, pieces, 0, fewest, window // WIDE, total)
+
+    def end_slice(index, tiles):
         def work(known):
             blocks = window // WIDE // 2**known
-            convolve_flat(stack(bank_ref[index], pieces), tiles, everyone, pieces, blocks, total)
+            convolve(
+                stack(bank_ref[index], pieces), tiles, everyone, pieces, fewest, blocks + pieces - 1, blocks, total
+            )
             widen(total, known, False)
 
         by_level(level_of(early + 1 + index), work)
 
+    begin_slice(0, tiles_ref.at[0])
+    for copy in tables:
+        copy.wait()
     for step in range(early + 1):
         by_level(level_of(step), functools.partial(widen, partial_ref.at[step], fresh=step == 0))
-    for index in range(ready):
-        one_slice(index, tiles_ref.at[index])
+    end_slice(0, tiles_ref.at[0])
+    for index in range(1, ready):
+        begin_slice(index, tiles_ref.at[index])
+        end_slice(index, tiles_ref.at[index])
     if late > ready:
         def rest(index, carry):
             fill(
                 lambda det, at: series_ref[(index - ready) * dets + det, :, pl.ds(at, LANES)],
                 squares[0], everyone, length // LANES,
             )
-            one_slice(index, squares[0])
+            begin_slice(index, squares[0])
+            end_slice(index, squares[0])
             return carry
 
         lax.fori_loop(ready, late, rest, 0)
@@ -424,7 +407,7 @@
             return jnp.maximum(highest, jnp.abs(summed))
 
         best[first : first + CHUNK] = lax.fori_loop(
-            0, delays_ref.shape[1], direction, jnp.zeros((CHUNK, LANES), jnp.float32), unroll=16
+            0, delays_ref.shape[1], direction, jnp.zeros((CHUNK, LANES), jnp.float32), unroll=32
         )
     for near in range(apart):
         back = best[near * LANES : (near + 1) * LANES].T
@@ -438,17 +421,21 @@
     ready = tiles.shape[0]
     dets = partial.shape[1]
     span = window // (LANES // rows)
-    smem = pl.BlockSpec(memory_space=pltpu.SMEM)
+    free = pl.BlockSpec(memory_space=pl.ANY)
     vmem = pl.BlockSpec(memory_space=pltpu.VMEM)
     return pl.pallas_call(
         functools.partial(search_kernel, early, ready),
         out_shape=jax.ShapeDtypeStruct((rows, window), jnp.float32),
-        in_specs=[smem, smem, smem, vmem, vmem, vmem, vmem],
+        in_specs=[free, free, free, vmem, vmem, vmem, vmem],
         out_specs=vmem,
         scratch_shapes=[
+            pltpu.SMEM(rates.shape, rates.dtype),
+            pltpu.SMEM(delays.shape, delays.dtype),
+            pltpu.SMEM(antenna.shape, antenna.dtype),
             pltpu.VMEM(partial.shape[1:], jnp.float32),
             pltpu.VMEM((dets, span + HALO, LANES), jnp.float32),
             pltpu.VMEM((span, LANES), jnp.float32),
+            pltpu.SemaphoreType.DMA((3,)),
         ] + [pltpu.VMEM(tiles.shape[1:], tiles.dtype)] * (late > ready),
         compiler_params=pltpu.CompilerParams(vmem_limit_bytes=GRANT),
     )(rates, delays, antenna, bank, series, partial, tiles)

time: 19.3 us -> 18.5 us (0.959)
  Pallas kernels: 19.2 us -> 18.4 us
    pallas_call x1, Pallas kernels: 13.1 us -> 12.6 us  [exchange(): pl.pallas_call(functools.partial(exchange_kernel, cuts, dets, early, read...]
    pallas_call x1, Pallas kernels: 6.06 us -> 5.78 us  [search(): pl.pallas_call(functools.partial(search_kernel, early, ready), out_shape=...]
where the time goes in v4:
time: 18.5 us; the launch traced here: 18.4 us
  Pallas kernels  18.4 us (99%)
    pallas_call x1, Pallas kernels, exchange(): pl.pallas_call(functools.partial(exchange_kernel, cuts, dets, early, read...  12.6 us
    pallas_call x1, Pallas kernels, search(): pl.pallas_call(functools.partial(search_kernel, early, ready), out_shape=...  5.78 us

profile of v4, /device:TPU:0, one launch (start us, length us, event | category | flops | bytes accessed | tf_op | source)
XLA Modules:
  0.0 18.4 jit_solution(871710517838880817)
XLA Ops:
  0.0 12.6 %shard_map.73 = (f32[1,16,2048]{2,1,0:T(8,128)S(1)}, f32[2,1,6144]{2,1,0:T(1,128)S(1)}, f32[3,2,32,16,128]{4,3,2,1,0:T(8,128)S(1)}, bf16[1,2,48,128,128]{4,3,2,1...) custom-call(s32[1,128]{1,0:T(1,128)} %bitcast.11, bf16[1,6144]{1,0:T(2,128)(2,1)} %bitcast.8, ...), custom_call_target="tpu_custom_call" | custom-call | tf_op jit(solution)/shard_map/pallas_call | solution.py:258
  12.6 5.8 %shard_map.74 = f32[16,4096]{1,0:T(8,128)} custom-call(s32[4]{0:T(128)S(1)} %get-tuple-element.12.rates_any, s32[2,64]{1,0:T(2,128)S(1)} %get-tuple-element.13.delays_any, f32[2,64]{1,0:T(2,128)S(1)} %get-tuple-element.14.antenna_any, f32[1,16,2048]{2,1,0:T(8,128)S(1)} %get-tuple-element.15.bank_ref, f32[2,1,6144]{2,1,0:T(1,128)S(1)} %get-tuple-element.16.series_ref, ...), custom_call_target="tpu_custom_call" | custom-call | tf_op jit(solution)/shard_map/pallas_call | solution.py:426

commit v5 on v4

--- a/solution.py
+++ b/solution.py
@@ -9,6 +9,7 @@
 
 MESH = pl.DeviceIdType.MESH
 LANES = 128
+SUBLANES = 8
 WIDE = 256
 DEEP = 48
 COARSEST = 8
@@ -229,11 +230,14 @@
         forward(step)
     for step in range(early + 1, held + 1):
         prepare(step, core)
-    for step in range(1, held + 1):
+    for step in range(1, early + 1):
         prepare_others(step)
     for step in range(1, early + 1):
         banks[step - 1].wait_recv()
         filtered(step, bank_early[step - 1])
+        if step == 1:
+            for late in range(early + 1, held + 1):
+                prepare_others(late)
     for copy in fetches[4:]:
         copy.wait()
     for copy in side[(held + 1) * (dets - 1) :]:
@@ -292,7 +296,7 @@
 
 def search_kernel(
     early, ready, rates_any, delays_any, antenna_any, bank_ref, series_ref, partial_ref, tiles_ref, peak_ref,
-    rates_ref, delays_ref, antenna_ref, total, turned, best, table_sem, *squares,
+    rates_ref, delays_ref, antenna_ref, total, turned, spread, best, table_sem, *squares,
 ):
     tables = [
         pltpu.make_async_copy(rates_any, rates_ref, table_sem.at[0]),
@@ -338,6 +342,13 @@
                 ))]
             for first, block in blocks:
                 size = block.shape[0]
+                if rate == SUBLANES:
+                    spread[det, :size] = block
+                    for row in range(size):
+                        place = pl.ds((first + row) * rate, rate)
+                        value = jnp.broadcast_to(spread[det, row : row + 1], (rate, LANES))
+                        turned[det, place, :] = value if fresh else turned[det, place, :] + value
+                    continue
                 for turn in range(rate):
                     if rate > 1:
                         place = pl.ds(first * rate + turn, size, stride=rate)
@@ -434,6 +445,7 @@
             pltpu.SMEM(antenna.shape, antenna.dtype),
             pltpu.VMEM(partial.shape[1:], jnp.float32),
             pltpu.VMEM((dets, span + HALO, LANES), jnp.float32),
+            pltpu.VMEM((dets, LANES, LANES), jnp.float32),
             pltpu.VMEM((span, LANES), jnp.float32),
             pltpu.SemaphoreType.DMA((3,)),
         ] + [pltpu.VMEM(tiles.shape[1:], tiles.dtype)] * (late > ready),

time: 18.5 us -> 18.4 us (level)
  no operation moved by 1% of the time
where the time goes in v5:
time: 18.4 us; the launch traced here: 18.3 us
  Pallas kernels  18.3 us (99%)
    pallas_call x1, Pallas kernels, exchange(): pl.pallas_call(functools.partial(exchange_kernel, cuts, dets, early, read...  12.6 us
    pallas_call x1, Pallas kernels, search(): pl.pallas_call(functools.partial(search_kernel, early, ready), out_shape=...  5.66 us

profile of v5, /device:TPU:0, one launch (start us, length us, event | category | flops | bytes accessed | tf_op | source)
XLA Modules:
  0.0 18.3 jit_solution(5827865843044849746)
XLA Ops:
  0.0 12.6 %shard_map.73 = (f32[1,16,2048]{2,1,0:T(8,128)S(1)}, f32[2,1,6144]{2,1,0:T(1,128)S(1)}, f32[3,2,32,16,128]{4,3,2,1,0:T(8,128)S(1)}, bf16[1,2,48,128,128]{4,3,2,1...) custom-call(s32[1,128]{1,0:T(1,128)} %bitcast.11, bf16[1,6144]{1,0:T(2,128)(2,1)} %bitcast.8, ...), custom_call_target="tpu_custom_call" | custom-call | tf_op jit(solution)/shard_map/pallas_call | solution.py:262
  12.6 5.7 %shard_map.74 = f32[16,4096]{1,0:T(8,128)} custom-call(s32[4]{0:T(128)S(1)} %get-tuple-element.12.rates_any, s32[2,64]{1,0:T(2,128)S(1)} %get-tuple-element.13.delays_any, f32[2,64]{1,0:T(2,128)S(1)} %get-tuple-element.14.antenna_any, f32[1,16,2048]{2,1,0:T(8,128)S(1)} %get-tuple-element.15.bank_ref, f32[2,1,6144]{2,1,0:T(1,128)S(1)} %get-tuple-element.16.series_ref, ...), custom_call_target="tpu_custom_call" | custom-call | tf_op jit(solution)/shard_map/pallas_call | solution.py:437

commit v6 on v4

--- a/solution.py
+++ b/solution.py
@@ -13,7 +13,7 @@
 DEEP = 48
 COARSEST = 8
 HALO = 48
-CHUNK = 64
+CHUNK = 128
 EARLY = 2
 READY = 1
 GRANT = 24 * 2**20
@@ -407,7 +407,7 @@
             return jnp.maximum(highest, jnp.abs(summed))
 
         best[first : first + CHUNK] = lax.fori_loop(
-            0, delays_ref.shape[1], direction, jnp.zeros((CHUNK, LANES), jnp.float32), unroll=32
+            0, delays_ref.shape[1], direction, jnp.zeros((CHUNK, LANES), jnp.float32), unroll=16
         )
     for near in range(apart):
         back = best[near * LANES : (near + 1) * LANES].T

time: 18.5 us -> 18.4 us (level)
  no operation moved by 1% of the time
where the time goes in v6:
time: 18.4 us; the launch traced here: 18.3 us
  Pallas kernels  18.3 us (99%)
    pallas_call x1, Pallas kernels, exchange(): pl.pallas_call(functools.partial(exchange_kernel, cuts, dets, early, read...  12.6 us
    pallas_call x1, Pallas kernels, search(): pl.pallas_call(functools.partial(search_kernel, early, ready), out_shape=...  5.68 us

profile of v6, /device:TPU:0, one launch (start us, length us, event | category | flops | bytes accessed | tf_op | source)
XLA Modules:
  0.0 18.3 jit_solution(7063368898704780336)
XLA Ops:
  0.0 12.6 %shard_map.73 = (f32[1,16,2048]{2,1,0:T(8,128)S(1)}, f32[2,1,6144]{2,1,0:T(1,128)S(1)}, f32[3,2,32,16,128]{4,3,2,1,0:T(8,128)S(1)}, bf16[1,2,48,128,128]{4,3,2,1...) custom-call(s32[1,128]{1,0:T(1,128)} %bitcast.11, bf16[1,6144]{1,0:T(2,128)(2,1)} %bitcast.8, ...), custom_call_target="tpu_custom_call" | custom-call | tf_op jit(solution)/shard_map/pallas_call | solution.py:258
  12.6 5.7 %shard_map.74 = f32[16,4096]{1,0:T(8,128)} custom-call(s32[4]{0:T(128)S(1)} %get-tuple-element.12.rates_any, s32[2,64]{1,0:T(2,128)S(1)} %get-tuple-element.13.delays_any, f32[2,64]{1,0:T(2,128)S(1)} %get-tuple-element.14.antenna_any, f32[1,16,2048]{2,1,0:T(8,128)S(1)} %get-tuple-element.15.bank_ref, f32[2,1,6144]{2,1,0:T(1,128)S(1)} %get-tuple-element.16.series_ref, ...), custom_call_target="tpu_custom_call" | custom-call | tf_op jit(solution)/shard_map/pallas_call | solution.py:426

commit v7 on v5

--- a/solution.py
+++ b/solution.py
@@ -230,14 +230,11 @@
         forward(step)
     for step in range(early + 1, held + 1):
         prepare(step, core)
-    for step in range(1, early + 1):
+    for step in range(1, held + 1):
         prepare_others(step)
     for step in range(1, early + 1):
         banks[step - 1].wait_recv()
         filtered(step, bank_early[step - 1])
-        if step == 1:
-            for late in range(early + 1, held + 1):
-                prepare_others(late)
     for copy in fetches[4:]:
         copy.wait()
     for copy in side[(held + 1) * (dets - 1) :]:

time: 18.4 us -> 18.4 us (level)
  no operation moved by 1% of the time
where the time goes in v7:
time: 18.4 us; the launch traced here: 18.3 us
  Pallas kernels  18.3 us (99%)
    pallas_call x1, Pallas kernels, exchange(): pl.pallas_call(functools.partial(exchange_kernel, cuts, dets, early, read...  12.6 us
    pallas_call x1, Pallas kernels, search(): pl.pallas_call(functools.partial(search_kernel, early, ready), out_shape=...  5.65 us

profile of v7, /device:TPU:0, one launch (start us, length us, event | category | flops | bytes accessed | tf_op | source)
XLA Modules:
  0.0 18.3 jit_solution(4424832769348094223)
XLA Ops:
  0.0 12.6 %shard_map.73 = (f32[1,16,2048]{2,1,0:T(8,128)S(1)}, f32[2,1,6144]{2,1,0:T(1,128)S(1)}, f32[3,2,32,16,128]{4,3,2,1,0:T(8,128)S(1)}, bf16[1,2,48,128,128]{4,3,2,1...) custom-call(s32[1,128]{1,0:T(1,128)} %bitcast.11, bf16[1,6144]{1,0:T(2,128)(2,1)} %bitcast.8, ...), custom_call_target="tpu_custom_call" | custom-call | tf_op jit(solution)/shard_map/pallas_call | solution.py:259
  12.6 5.6 %shard_map.74 = f32[16,4096]{1,0:T(8,128)} custom-call(s32[4]{0:T(128)S(1)} %get-tuple-element.12.rates_any, s32[2,64]{1,0:T(2,128)S(1)} %get-tuple-element.13.delays_any, f32[2,64]{1,0:T(2,128)S(1)} %get-tuple-element.14.antenna_any, f32[1,16,2048]{2,1,0:T(8,128)S(1)} %get-tuple-element.15.bank_ref, f32[2,1,6144]{2,1,0:T(1,128)S(1)} %get-tuple-element.16.series_ref, ...), custom_call_target="tpu_custom_call" | custom-call | tf_op jit(solution)/shard_map/pallas_call | solution.py:434
